TPU v7x, 512 devices: a whole 4x4x16 slice. The times are simulated.
512 devices in a mesh: rep: 8 (over y, core), exp: 64 (over x, z).
Axes of the slice: x: 4, y: 4, z: 16, core: 2. Of those that a mesh axis runs over, the one named last changes fastest.
Arguments:
- payload: bfloat16 [16384, 2048], P(('rep', 'exp')), may hold values from -6 to 6
- block_scales: bfloat16 [16384, 16], P(('rep', 'exp')), may hold values from 0.29882812 to 3
- cotangent: bfloat16 [16384, 2048], P(('rep', 'exp')), may hold values from -12 to 12
- expert_ids: int32 [16384, 8], P(('rep', 'exp')), may hold values from 0 to 63, all different within a row; in each aligned block of 32 rows (0 to 31, 32 to 63, ...) at most 5 rows name the same one
- route_counts: int32 [16384, 8], P(('rep', 'exp')), may hold values from 1 to 15
- gate_up: bfloat16 [64, 2, 2048, 384], P('exp', None, 'rep'), may hold values from -0.125 to 0.125
- down_weight: bfloat16 [64, 384, 2048], P('exp', None, 'rep'), may hold values from -0.3125 to 0.3125
- first_moment: float32 [64, 2, 2048, 384], P('exp', None, 'rep'), may hold values from -12 to 12
- second_moment: float32 [64, 2, 2048, 384], P('exp', None, 'rep'), may hold values from 10 to 300
Outputs:
- d_activation: bfloat16 [16384, 2048], P(('rep', 'exp'))
- new_first: float32 [64, 2, 2048, 384], P('exp', None, 'rep')
- new_second: float32 [64, 2, 2048, 384], P('exp', None, 'rep')
- weight_step: bfloat16 [64, 2, 2048, 384], P('exp', None, 'rep')
Inputs may be any that keep to these rules, and one draw needn't show every extreme that they name: `expert_ids`: in the rows of one device (aligned blocks of 32 tokens) no expert is named more than 5 times, a bound that some block reaches; each token names 8 different experts.
All inputs are finite; a program needn't handle non-finite values.
Results may differ from a plain program's by a relative error of at most 0.02.
Values may be sent and summed in bfloat16 or wider, within the bound.
A program may use at most 64 MiB of HBM per device.

v0:
```python
import jax
import jax.numpy as jnp
import numpy as np
from jax import lax
from jax.sharding import PartitionSpec as P

X_SIZE = 4
Z_SIZE = 16
CAPACITY = 5
Z_GROUPS = [[x * Z_SIZE + z for z in range(Z_SIZE)] for x in range(X_SIZE)]
X_GROUPS = [[x * Z_SIZE + z for x in range(X_SIZE)] for z in range(Z_SIZE)]


def silu_parts(gate_pre):
    sigmoid_val = jax.nn.sigmoid(gate_pre)
    return (gate_pre * sigmoid_val, sigmoid_val * (1.0 + gate_pre * (1.0 - sigmoid_val)))


def dequantize(values, scales):
    array_shape = values.shape
    blocked = values.astype(jnp.float32).reshape(
        array_shape[:-1] + (scales.shape[-1], array_shape[-1] // scales.shape[-1])
    )
    return (
        (blocked * scales.astype(jnp.float32)[..., None]).reshape(array_shape).astype(jnp.bfloat16)
    )


def route_tables(ids, counts, z_pos, tok_rows):
    count_float = counts.astype(jnp.float32)
    share = count_float / jnp.sum(count_float, axis=1, keepdims=True)
    experts = jnp.arange(X_SIZE, dtype=jnp.int32) * Z_SIZE + z_pos
    hit = ids[None] == experts[:, None, None]
    match = jnp.any(hit, axis=2)
    weight = jnp.sum(jnp.where(hit, share[None], 0.0), axis=2)
    ones = match.astype(jnp.bfloat16).reshape(X_SIZE * Z_SIZE, tok_rows)
    before = jnp.asarray(np.triu(np.ones((tok_rows, tok_rows)), 1), jnp.bfloat16)
    rank = jnp.dot(ones, before, preferred_element_type=jnp.float32).astype(jnp.int32)
    base = jnp.arange(Z_SIZE, dtype=jnp.int32)[None, :, None] * CAPACITY
    slot = (base + rank.reshape(X_SIZE, Z_SIZE, tok_rows)).reshape(X_SIZE, Z_SIZE * tok_rows)
    slot = jnp.where(match, slot, -1)
    lanes = jnp.arange(Z_SIZE * CAPACITY, dtype=jnp.int32)
    pick = slot[:, None, :] == lanes[None, :, None]
    slot_share = jnp.sum(jnp.where(pick, weight[:, None, :], 0.0), axis=2)
    pick = pick.reshape(X_SIZE * Z_SIZE * CAPACITY, Z_SIZE * tok_rows).astype(jnp.bfloat16)
    return (pick, slot_share.reshape(X_SIZE * Z_SIZE * CAPACITY))


def on_device(
    payload,
    block_scales,
    cotangent,
    expert_ids,
    route_counts,
    gate_up,
    down_weight,
    first_moment,
    second_moment,
):
    tok_rows, width = payload.shape
    replicas = lax.axis_size("rep")
    z_pos = lax.axis_index("exp") % Z_SIZE
    side = Z_SIZE * CAPACITY
    slot_count = X_SIZE * side
    activation = dequantize(payload, block_scales)
    routing = jnp.concatenate([expert_ids, route_counts], axis=1).astype(jnp.bfloat16)
    routing = jnp.pad(routing, ((0, 0), (0, 112)))
    act_all = lax.all_gather(
        jnp.concatenate([activation, routing], axis=1),
        "exp",
        axis=0,
        tiled=True,
        axis_index_groups=Z_GROUPS,
    )
    cot_all = lax.all_gather(cotangent, "exp", axis=0, tiled=True, axis_index_groups=Z_GROUPS)
    whole_gate_up = lax.all_gather(gate_up, "rep", axis=2, tiled=True)
    whole_down = lax.all_gather(down_weight, "rep", axis=2, tiled=True)
    top = expert_ids.shape[1]
    ids = act_all[:, width : width + top].astype(jnp.int32)
    counts = act_all[:, width + top : width + 2 * top].astype(jnp.int32)
    pick, slot_share = route_tables(ids, counts, z_pos, tok_rows)

    def to_experts(rows):
        return lax.all_to_all(
            rows.reshape(X_SIZE, side, width),
            "exp",
            split_axis=0,
            concat_axis=0,
            tiled=True,
            axis_index_groups=X_GROUPS,
        )

    act_rows = jnp.dot(pick, act_all[:, :width], preferred_element_type=jnp.float32)
    input_rows = to_experts(act_rows.astype(jnp.bfloat16)).reshape(slot_count, width)
    cot_rows = jnp.dot(pick, cot_all, preferred_element_type=jnp.float32)
    cot_rows = (slot_share[:, None] * cot_rows).astype(jnp.bfloat16)
    cotan_rows = to_experts(cot_rows).reshape(slot_count, width)
    pre_acts = jnp.einsum(
        "sd,tdf->tsf", input_rows, whole_gate_up[0], preferred_element_type=jnp.float32
    )
    hidden_grad = jnp.einsum(
        "sd,fd->sf", cotan_rows, whole_down[0], preferred_element_type=jnp.float32
    )
    silu_val, silu_slope = silu_parts(pre_acts[0])
    gate_grad = (hidden_grad * pre_acts[1] * silu_slope).astype(jnp.bfloat16)
    up_grad = (hidden_grad * silu_val).astype(jnp.bfloat16)
    row_grad = (
        jnp.einsum("sf,df->sd", gate_grad, whole_gate_up[0, 0], preferred_element_type=jnp.float32)
        + jnp.einsum("sf,df->sd", up_grad, whole_gate_up[0, 1], preferred_element_type=jnp.float32)
    ).astype(jnp.bfloat16)
    home = to_experts(row_grad).reshape(slot_count, width)
    partial = jnp.einsum("st,sd->td", pick, home, preferred_element_type=jnp.float32)
    d_activation = lax.psum_scatter(
        partial.astype(jnp.bfloat16),
        "exp",
        scatter_dimension=0,
        tiled=True,
        axis_index_groups=Z_GROUPS,
    )
    hidden_width = gate_grad.shape[1]
    both_grads = jnp.concatenate([gate_grad, up_grad], axis=1)
    term = jnp.einsum("sd,sf->df", input_rows, both_grads, preferred_element_type=jnp.float32)
    term = lax.optimization_barrier(term.astype(jnp.bfloat16))
    local_square = jnp.sum(jnp.square(term.astype(jnp.float32)))
    summed = lax.psum_scatter(term, "rep", scatter_dimension=0, tiled=True).astype(jnp.float32)
    shard_rows = width // replicas
    grad_shard = summed.reshape(shard_rows, 2, hidden_width).transpose(1, 0, 2)
    small_sum, big_sum = lax.psum((local_square, jnp.sum(jnp.square(grad_shard))), "rep")
    entry_count = 2.0 * width * hidden_width
    small_norm = small_sum / (replicas * entry_count)
    big_norm = big_sum / (replicas * replicas * entry_count)
    noise_gain = replicas * big_norm / (small_norm + 1e-06)
    new_first = 0.9 * first_moment + 0.1 * grad_shard[None]
    new_second = 0.95 * second_moment + 0.05 * jnp.square(grad_shard[None])
    weight_step = (noise_gain * new_first / (jnp.sqrt(new_second) + 1e-08)).astype(jnp.bfloat16)
    return (d_activation, new_first, new_second, weight_step)


def solution(mesh):
    tokens = P(("rep", "exp"), None)
    shards = P("exp", None, "rep", None)
    return jax.shard_map(
        on_device,
        mesh=mesh,
        in_specs=(tokens,) * 5 + (shards, P("exp", None, "rep"), shards, shards),
        out_specs=(tokens, shards, shards, shards),
        check_vma=False,
    )
```

profile of v0, /device:TPU:6, one launch (start us, length us, event | category | flops | bytes accessed | tf_op | source)
XLA Modules:
  0.0 364.9 jit_solution(17802854460447803655)
XLA Ops:
  7.2 0.0 copy-start.6
  7.2 0.0 all-gather.5.cloned.1.call-start
  7.2 0.8 copy.36
  8.0 0.8 copy.35
  8.8 0.8 copy.34
  9.5 0.1 fusion.26
  9.6 0.1 mul.102
  9.7 1.0 fusion.22
  10.7 0.7 pad_maximum_fusion
  11.4 0.0 all-gather.5.cloned.1.call-update
  11.4 0.0 all-gather.7.cloned.1.call-start
  11.5 0.7 all-gather.7.cloned.1.call-update
  12.2 0.0 all-gather.11.cloned.1.call-start
  12.2 0.7 all-gather.11.cloned.1.call-update
  12.9 0.0 all-gather.9.cloned.1.call-start
  13.0 0.5 all-gather.9.cloned.1.call-update
  13.5 0.1 eq.47
  13.6 0.1 add.68
  13.7 0.1 add.69
  13.8 75.3 %all-gather.5.cloned.1.call-done = bf16[512,2176]{1,0:T(8,128)(2,1)} async-done(((bf16[32,2176]{1,0:T(8,128)(2,1)}), bf16[512,2176]{1,0:T(8,128)(2,1)}) %all-gather.5.cloned.1.call-update) | async-done | bytes 2228240 | tf_op jit(solution)/shard_map/all_gather | solution.py:68
  89.0 1.1 fusion.30
  90.1 0.1 copy.42
  90.2 0.1 compare_reduce_fusion
  90.3 0.1 reshape.85
  90.4 0.0 copy-done.6
  90.4 0.2 convolution_convert_fusion.2
  90.6 0.1 copy.38
  90.7 0.1 reshape.86
  90.8 0.2 bitcast_compare_fusion
  91.0 3.5 convolution_convert_fusion.1
  94.5 4.8 %all-to-all-start.1 = ((bf16[4,80,2048]{2,1,0:T(8,128)(2,1)}), bf16[4,80,2048]{2,1,0:T(8,128)(2,1)S(1)}, u32[]{:S(2)}, u32[]{:S(2)}) async-start(bf16[4,80,2048]{2,1,0:T(8,128)(2,1)} %bitcast.4), calls=%async_computation.1 | async-start | bytes 2621440 | tf_op jit(solution)/shard_map/all_to_all | solution.py:84
  99.3 0.1 copy.43
  99.4 0.1 fusion.23
  99.5 0.2 select_reduce_fusion
  99.6 0.1 mul.107
  99.7 61.3 %all-gather.7.cloned.1.call-done = bf16[512,2048]{1,0:T(8,128)(2,1)} async-done(((bf16[32,2048]{1,0:T(8,128)(2,1)}), bf16[512,2048]{1,0:T(8,128)(2,1)}) %all-gather.7.cloned.1.call-update) | async-done | bytes 2097168 | tf_op jit(solution)/shard_map/all_gather | solution.py:75
  161.0 3.5 fusion.3
  164.5 0.0 all-to-all-done.1
  164.5 4.8 %all-to-all-start = ((bf16[4,80,2048]{2,1,0:T(8,128)(2,1)}), bf16[4,80,2048]{2,1,0:T(8,128)(2,1)S(1)}, u32[]{:S(2)}, u32[]{:S(2)}) async-start(bf16[4,80,2048]{2,1,0:T(8,128)(2,1)} %bitcast.1), calls=%async_computation | async-start | bytes 2621440 | tf_op jit(solution)/shard_map/all_to_all | solution.py:84
  169.3 0.0 reduce-scatter.5.cloned.1.call-start
  169.3 26.2 %all-gather.11.cloned.1.call-done = bf16[1,2,2048,384]{3,2,1,0:T(8,128)(2,1)} async-done(((bf16[1,2,256,384]{3,2,1,0:T(8,128)(2,1)}), bf16[1,2,2048,384]{3,2,1,0:T(8,128)(2,1)}) %all-gather.11.cloned.1.call-update) | async-done | bytes 3145744 | tf_op jit(solution)/shard_map/all_gather | solution.py:76
  195.5 4.0 %fusion.8 = f32[2,320,384]{2,1,0:T(8,128)} fusion(bf16[320,2048,1]{1,0,2:T(8,128)(2,1)S(1)} %bitcast.88, bf16[1,2,2048,384]{3,2,1,0:T(8,128)(2,1)} %all-gather.11.cloned.1.call-done), kind=kOutput, calls=%fused_computation.16 | convolution fusion | flops 1006632960 | bytes 5439488 | tf_op jit(solution)/shard_map/sd,tdf->tsf/dot_general | solution.py:98
  199.5 30.6 %all-gather.9.cloned.1.call-done = bf16[1,384,2048]{2,1,0:T(8,128)(2,1)} async-done(((bf16[1,384,256]{2,1,0:T(8,128)(2,1)}), bf16[1,384,2048]{2,1,0:T(8,128)(2,1)}) %all-gather.9.cloned.1.call-update) | async-done | bytes 1572880 | tf_op jit(solution)/shard_map/all_gather | solution.py:77
  230.1 0.0 all-to-all-done
  230.1 2.6 multiply_convert_fusion
  232.7 0.0 copy-start.4
  232.7 0.7 copy-done.4
  233.4 3.5 convolution_convert_fusion
  236.9 0.0 reduce-scatter.5.cloned.1.call-update
  236.9 0.0 reduce-scatter.3.cloned.1.call-start
  237.0 1.8 copy-done.1
  238.8 0.9 fusion.5
  239.7 0.1 copy-done.5
  239.7 0.9 fusion.2
  240.6 20.8 %all_to_all.15 = bf16[4,80,2048]{2,1,0:T(8,128)(2,1)S(1)} all-to-all(bf16[4,80,2048]{2,1,0:T(8,128)(2,1)S(1)} %bitcast.85), channel_id=1, replica_groups={{0,16,32,48},{1,17,33,49},{2,18,34,50},{3,19,35,51},{4,20,36,52},{5,21,..., dimensions={0} | all-to-all | bytes 2621440 | tf_op jit(solution)/shard_map/all_to_all | solution.py:84
  261.5 2.7 bitcast_convert_fusion
  264.1 0.0 reduce-scatter.3.cloned.1.call-update
  264.1 0.0 copy-done
  264.1 2.2 multiply_reduce_fusion
  266.4 15.5 %reduce-scatter.5.cloned.1.call-done = bf16[256,768]{1,0:T(8,128)(2,1)} async-done(((bf16[2048,768]{1,0:T(8,128)(2,1)}), bf16[256,768]{1,0:T(8,128)(2,1)}) %reduce-scatter.5.cloned.1.call-update) | async-done | bytes 393232 | tf_op jit(solution)/shard_map/reduce_scatter | solution.py:125
  281.8 1.8 convert_multiply_fusion.1
  283.6 13.5 %all-reduce.1 = (f32[]{:T(128)}, f32[]{:T(128)}) all-reduce(f32[]{:T(128)} %get-tuple-element.14, f32[]{:T(128)} %multiply_reduce_fusion), channel_id=1, replica_groups=mesh['rep'=8,'exp'=64] {'rep'}, use_global_device_ids=true, to_apply=%region_7.8 | all-reduce | flops 2 | bytes 16 | tf_op jit(solution)/shard_map/psum | solution.py:128
  298.5 1.4 divide_convert_fusion
  300.0 58.1 %reduce-scatter.3.cloned.1.call-done = bf16[32,2048]{1,0:T(8,128)(2,1)} async-done(((bf16[512,2048]{1,0:T(8,128)(2,1)}), bf16[32,2048]{1,0:T(8,128)(2,1)}) %reduce-scatter.3.cloned.1.call-update) | async-done | bytes 131088 | tf_op jit(solution)/shard_map/reduce_scatter | solution.py:113
  (16 shorter events, 0.1 us)
Async XLA Ops:
  7.2 83.3 %copy-start.6 = (bf16[32,32]{1,0:T(8,128)(2,1)S(1)}, bf16[32,32]{1,0:T(8,128)(2,1)}, u32[]{:S(2)}) copy-start(bf16[32,32]{1,0:T(8,128)(2,1)} %constant.52.clone) | copy-start | bytes 6148
  7.2 81.9 %all-gather.5.cloned.1.call-start = ((), (), s32[]{:S(2)}) async-start(), calls=%async_computation.5 | async-start | bytes 2367488 | tf_op jit(solution)/shard_map/all_gather | solution.py:68
  11.4 149.6 %all-gather.7.cloned.1.call-start = ((), (), s32[]{:S(2)}) async-start(), calls=%async_computation.6 | async-start | bytes 2228224 | tf_op jit(solution)/shard_map/all_gather | solution.py:75
  12.2 183.3 %all-gather.11.cloned.1.call-start = ((), (), s32[]{:S(2)}) async-start(), calls=%async_computation.8 | async-start | bytes 3538944 | tf_op jit(solution)/shard_map/all_gather | solution.py:76
  12.9 217.2 %all-gather.9.cloned.1.call-start = ((), (), s32[]{:S(2)}) async-start(), calls=%async_computation.7 | async-start | bytes 1769472 | tf_op jit(solution)/shard_map/all_gather | solution.py:77
  94.5 70.1 %all-to-all-start.1 = ((bf16[4,80,2048]{2,1,0:T(8,128)(2,1)}), bf16[4,80,2048]{2,1,0:T(8,128)(2,1)S(1)}, u32[]{:S(2)}, u32[]{:S(2)}) async-start(bf16[4,80,2048]{2,1,0:T(8,128)(2,1)} %bitcast.4), calls=%async_computation.1 | async-start | bytes 2621440 | tf_op jit(solution)/shard_map/all_to_all | solution.py:84
  164.5 65.6 %all-to-all-start = ((bf16[4,80,2048]{2,1,0:T(8,128)(2,1)}), bf16[4,80,2048]{2,1,0:T(8,128)(2,1)S(1)}, u32[]{:S(2)}, u32[]{:S(2)}) async-start(bf16[4,80,2048]{2,1,0:T(8,128)(2,1)} %bitcast.1), calls=%async_computation | async-start | bytes 2621440 | tf_op jit(solution)/shard_map/all_to_all | solution.py:84
  169.3 112.5 %reduce-scatter.5.cloned.1.call-start = ((), (), s32[]{:S(2)}) async-start(), calls=%async_computation.10 | async-start | bytes 3538944 | tf_op jit(solution)/shard_map/reduce_scatter | solution.py:125
  232.7 0.7 copy-start.4
  236.9 1.9 copy-start.1
  236.9 121.2 %reduce-scatter.3.cloned.1.call-start = ((), (), s32[]{:S(2)}) async-start(), calls=%async_computation.9 | async-start | bytes 2228224 | tf_op jit(solution)/shard_map/reduce_scatter | solution.py:113
  238.8 0.9 copy-start.5
  261.5 2.7 copy-start
  266.4 32.1 %copy-start.2 = (f32[1,2,256,384]{3,2,1,0:T(8,128)S(1)}, f32[1,2,256,384]{3,2,1,0:T(8,128)}, u32[]{:S(2)}) copy-start(f32[1,2,256,384]{3,2,1,0:T(8,128)} %param.18) | copy-start | bytes 2359300
  266.4 32.1 %copy-start.3 = (f32[1,2,256,384]{3,2,1,0:T(8,128)S(1)}, f32[1,2,256,384]{3,2,1,0:T(8,128)}, u32[]{:S(2)}) copy-start(f32[1,2,256,384]{3,2,1,0:T(8,128)} %param.17) | copy-start | bytes 2359300
Sparse Core Ops, SparseCore 0:
  11.6 77.4 all-gather.4
  91.1 69.8 all-gather.6
  163.2 32.2 all-gather.10
  197.4 32.5 all-gather.8
  237.0 44.7 reduce-scatter.4
  285.1 72.9 reduce-scatter.2
where the time goes:
time: 366 us; the launch traced here: 365 us
  waiting for transfers between devices  269 us (73%)
  blocking collectives  34.4 us (9%)
  matrix products  21.7 us (6%)
  between operations  15.6 us (4%)
  starting transfers between devices  9.77 us (3%)
  other arithmetic  7.83 us (2%)
  local copies, waits for them, and re-layouts  6.8 us (2%)
    all_gather x1, waiting for transfers between devices, on_device(): lax.all_gather(jnp.concatenate([activation, routing], axis=1), 'exp', axi...  75.3 us
    all_gather x1, waiting for transfers between devices, on_device(): lax.all_gather(cotangent, 'exp', axis=0, tiled=True, axis_index_groups=Z_...  61.3 us
    reduce_scatter x1, waiting for transfers between devices, on_device(): lax.psum_scatter(partial.astype(jnp.bfloat16), 'exp', scatter_dimension=0...  58.1 us
    all_gather x1, waiting for transfers between devices, on_device(): whole_down = lax.all_gather(down_weight, 'rep', axis=2, tiled=True)  30.6 us
    all_gather x1, waiting for transfers between devices, on_device(): whole_gate_up = lax.all_gather(gate_up, 'rep', axis=2, tiled=True)  26.2 us
    all_to_all x1, blocking collectives, to_experts(): lax.all_to_all(rows.reshape(X_SIZE, side, width), 'exp', split_axis=0, co...  20.8 us
    reduce_scatter x1, waiting for transfers between devices, on_device(): lax.psum_scatter(term, 'rep', scatter_dimension=0, tiled=True)  15.5 us
    psum x1, blocking collectives, on_device(): lax.psum((local_square, jnp.sum(jnp.square(grad_shard))), 'rep')  13.5 us
  transfers between devices with their start and end apart: 8, of which 6 were waited for; matrix products, arithmetic and copies ran while one was open for 6% of the time, Pallas kernels for 0%

commit v1 on v0

--- a/solution.py
+++ b/solution.py
@@ -74,7 +74,15 @@
     )
     cot_all = lax.all_gather(cotangent, "exp", axis=0, tiled=True, axis_index_groups=Z_GROUPS)
     whole_gate_up = lax.all_gather(gate_up, "rep", axis=2, tiled=True)
-    whole_down = lax.all_gather(down_weight, "rep", axis=2, tiled=True)
+    whole_down = jnp.concatenate(
+        lax.all_to_all(
+            jnp.stack(lax.axis_size("rep") * [down_weight], axis=0),
+            axis_name="rep",
+            split_axis=0,
+            concat_axis=0,
+        ),
+        2,
+    )
     top = expert_ids.shape[1]
     ids = act_all[:, width : width + top].astype(jnp.int32)
     counts = act_all[:, width + top : width + 2 * top].astype(jnp.int32)

time: 366 us -> 334 us (0.913)
  waiting for transfers between devices: 269 us -> 230 us
  starting transfers between devices: 9.77 us -> 14.3 us
    all_gather x1 -> x0, waiting for transfers between devices: 30.6 us -> none  [on_device(): whole_down = lax.all_gather(down_weight, 'rep', axis=2, tiled=True)]
    all_gather x1, waiting for transfers between devices: 75.3 us -> 68.9 us  [on_device(): lax.all_gather(jnp.concatenate([activation, routing], axis=1), 'exp', axi...]
    all_to_all x0 -> x1, starting transfers between devices: none -> 4.6 us  [on_device(): lax.all_to_all(jnp.stack(lax.axis_size('rep') * [down_weight], axis=0), a...]
  transfers between devices with their start and end apart: 8 -> 8, of which waited for: 6 -> 5; matrix products, arithmetic and copies ran while one was open for 6% -> 8% of each run, Pallas kernels for 0% -> 0%
where the time goes in v1:
time: 334 us; the launch traced here: 333 us
  waiting for transfers between devices  230 us (69%)
  blocking collectives  34.3 us (10%)
  matrix products  21.8 us (7%)
  between operations  15.2 us (5%)
  starting transfers between devices  14.3 us (4%)
  local copies, waits for them, and re-layouts  9.27 us (3%)
  other arithmetic  7.83 us (2%)
    all_gather x1, waiting for transfers between devices, on_device(): lax.all_gather(jnp.concatenate([activation, routing], axis=1), 'exp', axi...  68.9 us
    all_gather x1, waiting for transfers between devices, on_device(): lax.all_gather(cotangent, 'exp', axis=0, tiled=True, axis_index_groups=Z_...  61.1 us
    reduce_scatter x1, waiting for transfers between devices, on_device(): lax.psum_scatter(partial.astype(jnp.bfloat16), 'exp', scatter_dimension=0...  58 us
    all_gather x1, waiting for transfers between devices, on_device(): whole_gate_up = lax.all_gather(gate_up, 'rep', axis=2, tiled=True)  26 us
    all_to_all x1, blocking collectives, to_experts(): lax.all_to_all(rows.reshape(X_SIZE, side, width), 'exp', split_axis=0, co...  20.8 us
    reduce_scatter x1, waiting for transfers between devices, on_device(): lax.psum_scatter(term, 'rep', scatter_dimension=0, tiled=True)  14.5 us
    psum x1, blocking collectives, on_device(): lax.psum((local_square, jnp.sum(jnp.square(grad_shard))), 'rep')  13.5 us
    all_to_all x2, starting transfers between devices, to_experts(): lax.all_to_all(rows.reshape(X_SIZE, side, width), 'exp', split_axis=0, co...  9.58 us
  transfers between devices with their start and end apart: 8, of which 5 were waited for; matrix products, arithmetic and copies ran while one was open for 8% of the time, Pallas kernels for 0%

profile of v1, /device:TPU:6, one launch (start us, length us, event | category | flops | bytes accessed | tf_op | source)
XLA Modules:
  0.0 332.8 jit_solution(13560788651903672731)
XLA Ops:
  7.2 0.0 all-gather.4.cloned.1.call-start
  7.2 0.8 copy.46
  8.0 0.8 copy.47
  8.7 0.8 copy.48
  9.5 0.1 fusion.24
  9.6 0.1 mul.102
  9.7 1.0 fusion.20
  10.7 0.7 pad_maximum_fusion
  11.4 0.0 all-gather.4.cloned.1.call-update
  11.4 0.0 all-gather.6.cloned.1.call-start
  11.5 0.7 all-gather.6.cloned.1.call-update
  12.2 0.0 all-gather.8.cloned.1.call-start
  12.2 0.7 all-gather.8.cloned.1.call-update
  12.9 1.1 copy.52
  14.0 1.4 stack.2
  15.4 4.6 %all-to-all-start.1 = ((bf16[8,1,384,256]{2,3,1,0:T(8,128)(2,1)}), bf16[8,1,384,256]{2,3,1,0:T(8,128)(2,1)S(1)}, u32[]{:S(2)}, u32[]{:S(2)}) async-start(bf16[8,1,384,256]{2,3,1,0:T(8,128)(2,1)} %stack.2), calls=%async_computation.1 | async-start | bytes 3145728 | tf_op jit(solution)/shard_map/all_to_all | solution.py:78
  20.0 0.1 eq.47
  20.1 0.1 add.68
  20.2 0.1 add.69
  20.2 68.9 %all-gather.4.cloned.1.call-done = bf16[512,2176]{1,0:T(8,128)(2,1)} async-done(((bf16[32,2176]{1,0:T(8,128)(2,1)}), bf16[512,2176]{1,0:T(8,128)(2,1)}) %all-gather.4.cloned.1.call-update) | async-done | bytes 2228240 | tf_op jit(solution)/shard_map/all_gather | solution.py:68
  89.1 1.1 fusion.28
  90.2 0.1 copy.56
  90.3 0.1 compare_reduce_fusion
  90.4 0.1 reshape.91
  90.5 0.0 copy-done.6
  90.5 0.2 convolution_convert_fusion.2
  90.7 0.1 copy.50
  90.8 0.1 reshape.92
  90.9 0.2 bitcast_compare_fusion
  91.0 3.5 %convolution_convert_fusion.1 = bf16[320,2048]{1,0:T(8,128)(2,1)} fusion(pred[320,512]{1,0:T(32,128)(4,1)S(1)} %bitcast_compare_fusion, bf16[512,2176]{1,0:T(8,128)(2,1)} %all-gather.4.cloned.1.call-done), kind=kOutput, calls=%fused_computation.9 | convolution fusion | flops 671744000 | bytes 3571712 | tf_op jit(solution)/shard_map/dot_general | solution.py:101
  94.5 0.0 all-to-all-done.1
  94.5 4.8 %all-to-all-start.2 = ((bf16[4,80,2048]{2,1,0:T(8,128)(2,1)}), bf16[4,80,2048]{2,1,0:T(8,128)(2,1)S(1)}, u32[]{:S(2)}, u32[]{:S(2)}) async-start(bf16[4,80,2048]{2,1,0:T(8,128)(2,1)} %bitcast.93), calls=%async_computation.2 | async-start | bytes 2621440 | tf_op jit(solution)/shard_map/all_to_all | solution.py:92
  99.3 0.1 copy.57
  99.5 0.1 fusion.21
  99.6 0.2 select_reduce_fusion
  99.7 0.1 mul.107
  99.8 61.1 %all-gather.6.cloned.1.call-done = bf16[512,2048]{1,0:T(8,128)(2,1)} async-done(((bf16[32,2048]{1,0:T(8,128)(2,1)}), bf16[512,2048]{1,0:T(8,128)(2,1)}) %all-gather.6.cloned.1.call-update) | async-done | bytes 2097168 | tf_op jit(solution)/shard_map/all_gather | solution.py:75
  160.9 3.6 %fusion.3 = bf16[320,2048]{1,0:T(8,128)(2,1)} fusion(pred[320,512]{1,0:T(32,128)(4,1)S(1)} %bitcast_compare_fusion, bf16[512,2048]{1,0:T(8,128)(2,1)} %all-gather.6.cloned.1.call-done, f32[320]{0:T(512)S(1)} %mul.107), kind=kOutput, calls=%fused_computation.8 | convolution fusion | flops 672399360 | bytes 3572992 | tf_op jit(solution)/shard_map/dot_general | solution.py:103
  164.5 0.0 all-to-all-done.2
  164.5 4.8 %all-to-all-start = ((bf16[4,80,2048]{2,1,0:T(8,128)(2,1)}), bf16[4,80,2048]{2,1,0:T(8,128)(2,1)}, u32[]{:S(2)}, u32[]{:S(2)}) async-start(bf16[4,80,2048]{2,1,0:T(8,128)(2,1)} %bitcast.94), calls=%async_computation | async-start | bytes 2621440 | tf_op jit(solution)/shard_map/all_to_all | solution.py:92
  169.3 0.0 reduce-scatter.5.cloned.1.call-start
  169.3 26.0 %all-gather.8.cloned.1.call-done = bf16[1,2,2048,384]{3,2,1,0:T(8,128)(2,1)} async-done(((bf16[1,2,256,384]{3,2,1,0:T(8,128)(2,1)}), bf16[1,2,2048,384]{3,2,1,0:T(8,128)(2,1)}) %all-gather.8.cloned.1.call-update) | async-done | bytes 3145744 | tf_op jit(solution)/shard_map/all_gather | solution.py:76
  195.4 4.0 %fusion.6 = f32[2,320,384]{2,1,0:T(8,128)} fusion(bf16[320,2048,1]{1,0,2:T(8,128)(2,1)S(1)} %bitcast.91, bf16[1,2,2048,384]{3,2,1,0:T(8,128)(2,1)} %all-gather.8.cloned.1.call-done), kind=kOutput, calls=%fused_computation.14 | convolution fusion | flops 1006632960 | bytes 5439488 | tf_op jit(solution)/shard_map/sd,tdf->tsf/dot_general | solution.py:106
  199.4 0.0 all-to-all-done
  199.4 2.5 multiply_convert_fusion
  201.9 0.0 copy-start.4
  201.9 0.7 copy-done.4
  202.6 3.5 %convolution_convert_fusion = bf16[2048,768]{1,0:T(8,128)(2,1)} fusion(bf16[320,2048]{1,0:T(8,128)(2,1)S(1)} %bitcast.92, bf16[320,384]{1,0:T(8,128)(2,1)S(1)} %get-tuple-element.11, bf16[320,384]{1,0:T(8,128)(2,1)S(1)} %get-tuple-element.12), kind=kOutput, calls=%fused_computation.2 | convolution fusion | flops 1009188864 | bytes 4947968 | tf_op jit(solution)/shard_map/sd,sf->df/dot_general | solution.py:130
  206.1 0.0 reduce-scatter.5.cloned.1.call-update
  206.2 0.0 reduce-scatter.3.cloned.1.call-start
  206.2 1.8 copy-done.1
  208.0 0.9 fusion.5
  208.9 0.1 copy-done.5
  209.0 0.9 fusion.2
  209.9 20.8 %all_to_all.20 = bf16[4,80,2048]{2,1,0:T(8,128)(2,1)S(1)} all-to-all(bf16[4,80,2048]{2,1,0:T(8,128)(2,1)S(1)} %bitcast.87), channel_id=1, replica_groups={{0,16,32,48},{1,17,33,49},{2,18,34,50},{3,19,35,51},{4,20,36,52},{5,21,..., dimensions={0} | all-to-all | bytes 2621440 | tf_op jit(solution)/shard_map/all_to_all | solution.py:92
  230.7 2.7 bitcast_convert_fusion
  233.4 0.0 reduce-scatter.3.cloned.1.call-update
  233.4 0.0 copy-done
  233.4 2.2 multiply_reduce_fusion
  235.6 14.5 %reduce-scatter.5.cloned.1.call-done = bf16[256,768]{1,0:T(8,128)(2,1)} async-done(((bf16[2048,768]{1,0:T(8,128)(2,1)}), bf16[256,768]{1,0:T(8,128)(2,1)}) %reduce-scatter.5.cloned.1.call-update) | async-done | bytes 393232 | tf_op jit(solution)/shard_map/reduce_scatter | solution.py:133
  250.1 1.8 convert_multiply_fusion.1
  251.9 13.5 %all-reduce.1 = (f32[]{:T(128)}, f32[]{:T(128)}) all-reduce(f32[]{:T(128)} %get-tuple-element.14, f32[]{:T(128)} %multiply_reduce_fusion), channel_id=1, replica_groups=mesh['rep'=8,'exp'=64] {'rep'}, use_global_device_ids=true, to_apply=%region_7.8 | all-reduce | flops 2 | bytes 16 | tf_op jit(solution)/shard_map/psum | solution.py:136
  266.8 1.4 divide_convert_fusion
  268.3 58.0 %reduce-scatter.3.cloned.1.call-done = bf16[32,2048]{1,0:T(8,128)(2,1)} async-done(((bf16[512,2048]{1,0:T(8,128)(2,1)}), bf16[32,2048]{1,0:T(8,128)(2,1)}) %reduce-scatter.3.cloned.1.call-update) | async-done | bytes 131088 | tf_op jit(solution)/shard_map/reduce_scatter | solution.py:121
  (17 shorter events, 0.1 us)
Async XLA Ops:
  7.2 81.9 %all-gather.4.cloned.1.call-start = ((), (), s32[]{:S(2)}) async-start(), calls=%async_computation.6 | async-start | bytes 2367488 | tf_op jit(solution)/shard_map/all_gather | solution.py:68
  11.4 149.5 %all-gather.6.cloned.1.call-start = ((), (), s32[]{:S(2)}) async-start(), calls=%async_computation.7 | async-start | bytes 2228224 | tf_op jit(solution)/shard_map/all_gather | solution.py:75
  12.2 183.2 %all-gather.8.cloned.1.call-start = ((), (), s32[]{:S(2)}) async-start(), calls=%async_computation.8 | async-start | bytes 3538944 | tf_op jit(solution)/shard_map/all_gather | solution.py:76
  15.4 75.1 %copy-start.6 = (bf16[32,32]{1,0:T(8,128)(2,1)S(1)}, bf16[32,32]{1,0:T(8,128)(2,1)}, u32[]{:S(2)}) copy-start(bf16[32,32]{1,0:T(8,128)(2,1)} %constant.52.clone) | copy-start | bytes 6148
  15.4 79.2 %all-to-all-start.1 = ((bf16[8,1,384,256]{2,3,1,0:T(8,128)(2,1)}), bf16[8,1,384,256]{2,3,1,0:T(8,128)(2,1)S(1)}, u32[]{:S(2)}, u32[]{:S(2)}) async-start(bf16[8,1,384,256]{2,3,1,0:T(8,128)(2,1)} %stack.2), calls=%async_computation.1 | async-start | bytes 3145728 | tf_op jit(solution)/shard_map/all_to_all | solution.py:78
  94.5 70.0 %all-to-all-start.2 = ((bf16[4,80,2048]{2,1,0:T(8,128)(2,1)}), bf16[4,80,2048]{2,1,0:T(8,128)(2,1)S(1)}, u32[]{:S(2)}, u32[]{:S(2)}) async-start(bf16[4,80,2048]{2,1,0:T(8,128)(2,1)} %bitcast.93), calls=%async_computation.2 | async-start | bytes 2621440 | tf_op jit(solution)/shard_map/all_to_all | solution.py:92
  164.5 34.9 %all-to-all-start = ((bf16[4,80,2048]{2,1,0:T(8,128)(2,1)}), bf16[4,80,2048]{2,1,0:T(8,128)(2,1)}, u32[]{:S(2)}, u32[]{:S(2)}) async-start(bf16[4,80,2048]{2,1,0:T(8,128)(2,1)} %bitcast.94), calls=%async_computation | async-start | bytes 2621440 | tf_op jit(solution)/shard_map/all_to_all | solution.py:92
  169.3 80.8 %reduce-scatter.5.cloned.1.call-start = ((), (), s32[]{:S(2)}) async-start(), calls=%async_computation.10 | async-start | bytes 3538944 | tf_op jit(solution)/shard_map/reduce_scatter | solution.py:133
  201.9 0.7 copy-start.4
  206.1 1.9 copy-start.1
  206.2 120.1 %reduce-scatter.3.cloned.1.call-start = ((), (), s32[]{:S(2)}) async-start(), calls=%async_computation.9 | async-start | bytes 2228224 | tf_op jit(solution)/shard_map/reduce_scatter | solution.py:121
  208.0 0.9 copy-start.5
  230.7 2.7 copy-start
  235.6 31.2 %copy-start.2 = (f32[1,2,256,384]{3,2,1,0:T(8,128)S(1)}, f32[1,2,256,384]{3,2,1,0:T(8,128)}, u32[]{:S(2)}) copy-start(f32[1,2,256,384]{3,2,1,0:T(8,128)} %param.18) | copy-start | bytes 2359300
  235.6 31.2 %copy-start.3 = (f32[1,2,256,384]{3,2,1,0:T(8,128)S(1)}, f32[1,2,256,384]{3,2,1,0:T(8,128)}, u32[]{:S(2)}) copy-start(f32[1,2,256,384]{3,2,1,0:T(8,128)} %param.17) | copy-start | bytes 2359300
Sparse Core Ops, SparseCore 0:
  11.5 77.5 all-gather.3
  91.2 69.6 all-gather.5
  163.1 32.2 all-gather.7
  206.3 43.8 reduce-scatter.4
  253.4 72.8 reduce-scatter.2
